TPU v7x, 32 devices: a whole 2x2x4 slice. The times are simulated.
32 devices in a mesh: seq: 16 (over z, y, x), chan: 2 (over core).
Axes of the slice: x: 2, y: 2, z: 4, core: 2. Of those that a mesh axis runs over, the one named last changes fastest.
Arguments:
- inputs: bfloat16 [1, 2048, 1024], P(None, 'seq', 'chan'), may hold values from -6 to 6
- decay: float32 [1024, 64], P('chan'), may hold values from 0.00024414062 to 0.03
- rotation: float32 [1024, 64], P('chan'), may hold values from -3.140625 to 3.140625
- in_proj: float32 [2, 1024, 64], P(None, 'chan'), may hold values from -6 to 6
- out_proj: float32 [2, 1024, 64], P(None, 'chan'), may hold values from -0.75 to 0.75
- low_rank: float32 [2, 1024, 64], P(None, 'chan'), may hold values from -6 to 6
- skip: float32 [1024], P('chan'), may hold values from -1 to 1
- mix_weight: bfloat16 [1024, 1024], P(None, 'chan'), may hold values from -0.1875 to 0.1875
Outputs:
- outputs: bfloat16 [1, 2048, 1024], P(None, 'seq', 'chan')
All inputs are finite; a program needn't handle non-finite values.
Results may differ from a plain program's by a relative error of at most 0.015.
Values may be sent and summed in bfloat16 or wider, within the bound.
A program may use at most 64 MiB of HBM per device.

v0:
```python
import functools
import math

import jax
import jax.numpy as jnp
import numpy as np
from jax import lax
from jax.experimental import pallas as pl
from jax.experimental.pallas import tpu as pltpu
from jax.sharding import PartitionSpec as P

MESH = pl.DeviceIdType.MESH
CHUNK = 16
PAIRS = CHUNK // 2
LANES = 128
f32 = jnp.float32
bf16 = jnp.bfloat16

highest = lax.Precision.HIGHEST


def cauchy_terms(decay, in_proj, out_proj, low_rank):
    scale = jnp.sqrt(2.0 * decay)
    in_real = scale * in_proj[0]
    in_imag = scale * in_proj[1]
    rank_real = scale * low_rank[0]
    rank_imag = scale * low_rank[1]
    out_real = out_proj[0]
    out_imag = out_proj[1]
    weight_real = jnp.stack(
        [
            out_real * in_real - out_imag * in_imag,
            out_real * rank_real - out_imag * rank_imag,
            rank_real * in_real + rank_imag * in_imag,
            rank_real * rank_real + rank_imag * rank_imag,
        ],
        axis=-1,
    )
    weight_imag = jnp.stack(
        [
            out_real * in_imag + out_imag * in_real,
            out_real * rank_imag + out_imag * rank_real,
            rank_real * in_imag - rank_imag * in_real,
            jnp.zeros_like(rank_real),
        ],
        axis=-1,
    )
    return (weight_real, weight_imag)


def spectrum_columns(omega, decay, rotation, weight_real, weight_imag):
    offset = omega[None, None, :] - rotation[:, :, None]
    magnitude = decay[:, :, None] * decay[:, :, None] + offset * offset
    factor_real = decay[:, :, None] / magnitude
    factor_imag = -offset / magnitude
    sums_real = jnp.einsum(
        "hnf,hnj->hjf", factor_real, weight_real, precision=highest
    ) - jnp.einsum("hnf,hnj->hjf", factor_imag, weight_imag, precision=highest)
    sums_imag = jnp.einsum(
        "hnf,hnj->hjf", factor_real, weight_imag, precision=highest
    ) + jnp.einsum("hnf,hnj->hjf", factor_imag, weight_real, precision=highest)
    numer_real = sums_real[:, 1] * sums_real[:, 2] - sums_imag[:, 1] * sums_imag[:, 2]
    numer_imag = sums_real[:, 1] * sums_imag[:, 2] + sums_imag[:, 1] * sums_real[:, 2]
    denom_real = 1.0 + sums_real[:, 3]
    denom_imag = sums_imag[:, 3]
    denom_size = denom_real * denom_real + denom_imag * denom_imag
    ratio_real = (numer_real * denom_real + numer_imag * denom_imag) / denom_size
    ratio_imag = (numer_imag * denom_real - numer_real * denom_imag) / denom_size
    return (sums_real[:, 0] - ratio_real, sums_imag[:, 0] - ratio_imag)


def blocked_spectrum(freq_index, length_all, decay, rotation, weight_real, weight_imag):
    freq_count = freq_index.shape[0]
    chan_width, states = decay.shape
    block = freq_count
    while block * chan_width * states > 262144 and block % 2 == 0 and (block > 128):
        block = block // 2

    def one_block(indices):
        signed = jnp.where(indices < length_all // 2, indices, indices - length_all)
        omega = signed.astype(jnp.float32) * (2.0 * math.pi / length_all)
        return spectrum_columns(omega, decay, rotation, weight_real, weight_imag)

    spec_real, spec_imag = lax.map(one_block, freq_index.reshape(freq_count // block, block))
    spec_real = jnp.transpose(spec_real, (0, 2, 1)).reshape(freq_count, chan_width)
    spec_imag = jnp.transpose(spec_imag, (0, 2, 1)).reshape(freq_count, chan_width)
    return (spec_real, spec_imag)


def general_device(inputs, decay, rotation, in_proj, out_proj, low_rank, skip, mix_weight):
    batches, local_len, chan_width = inputs.shape
    seq_count = lax.axis_size("seq")
    seq_index = lax.axis_index("seq")
    length_all = local_len * seq_count
    weight_real, weight_imag = cauchy_terms(decay, in_proj, out_proj, low_rank)
    small_index = jnp.arange(seq_count, dtype=jnp.int32)
    small_angle = (small_index[:, None] * small_index[None, :] % seq_count).astype(jnp.float32) * (
        2.0 * math.pi / seq_count
    )
    small_cos = jnp.cos(small_angle)
    small_sin = jnp.sin(small_angle)
    big_index = jnp.arange(local_len, dtype=jnp.int32)
    big_angle = (big_index[:, None] * big_index[None, :] % local_len).astype(jnp.float32) * (
        2.0 * math.pi / local_len
    )
    big_cos = jnp.cos(big_angle)
    big_sin = jnp.sin(big_angle)
    sub_width = chan_width // seq_count
    swapped = lax.all_to_all(
        inputs.reshape(batches, local_len, seq_count, sub_width),
        "seq",
        split_axis=2,
        concat_axis=1,
        tiled=True,
    )
    signal = swapped.astype(jnp.float32).reshape(batches, seq_count, local_len, sub_width)
    start = seq_index * sub_width
    my_decay = lax.dynamic_slice_in_dim(decay, start, sub_width, 0)
    my_rotation = lax.dynamic_slice_in_dim(rotation, start, sub_width, 0)
    my_wreal = lax.dynamic_slice_in_dim(weight_real, start, sub_width, 0)
    my_wimag = lax.dynamic_slice_in_dim(weight_imag, start, sub_width, 0)
    freq_grid = (small_index[:, None] + seq_count * big_index[None, :]).reshape(length_all)
    kern_real, kern_imag = blocked_spectrum(
        freq_grid, length_all, my_decay, my_rotation, my_wreal, my_wimag
    )
    kern_real = kern_real.reshape(seq_count, local_len, sub_width)[None]
    kern_imag = kern_imag.reshape(seq_count, local_len, sub_width)[None]
    first_real = jnp.einsum("ca,bamh->bcmh", small_cos, signal, precision=highest)
    first_imag = -jnp.einsum("ca,bamh->bcmh", small_sin, signal, precision=highest)
    twist_angle = (small_index[:, None] * big_index[None, :] % length_all).astype(jnp.float32) * (
        2.0 * math.pi / length_all
    )
    twist_cos = jnp.cos(twist_angle)[None, :, :, None]
    twist_sin = jnp.sin(twist_angle)[None, :, :, None]
    twisted_real = first_real * twist_cos + first_imag * twist_sin
    twisted_imag = first_imag * twist_cos - first_real * twist_sin
    freq_real = jnp.einsum("dm,bcmh->bcdh", big_cos, twisted_real, precision=highest) + jnp.einsum(
        "dm,bcmh->bcdh", big_sin, twisted_imag, precision=highest
    )
    freq_imag = jnp.einsum("dm,bcmh->bcdh", big_cos, twisted_imag, precision=highest) - jnp.einsum(
        "dm,bcmh->bcdh", big_sin, twisted_real, precision=highest
    )
    product_real = freq_real * kern_real - freq_imag * kern_imag
    product_imag = freq_real * kern_imag + freq_imag * kern_real
    back_real = jnp.einsum("md,bcdh->bcmh", big_cos, product_real, precision=highest) - jnp.einsum(
        "md,bcdh->bcmh", big_sin, product_imag, precision=highest
    )
    back_imag = jnp.einsum("md,bcdh->bcmh", big_cos, product_imag, precision=highest) + jnp.einsum(
        "md,bcdh->bcmh", big_sin, product_real, precision=highest
    )
    reverted_real = back_real * twist_cos - back_imag * twist_sin
    reverted_imag = back_imag * twist_cos + back_real * twist_sin
    conv = (
        jnp.einsum("ac,bcmh->bamh", small_cos, reverted_real, precision=highest)
        - jnp.einsum("ac,bcmh->bamh", small_sin, reverted_imag, precision=highest)
    ) * (1.0 / length_all)
    home = lax.all_to_all(
        conv.reshape(batches, length_all, 1, sub_width).astype(jnp.bfloat16),
        "seq",
        split_axis=1,
        concat_axis=2,
        tiled=True,
    ).astype(jnp.float32)
    home = home.reshape(batches, local_len, chan_width)
    mixed_in = home + skip[None, None, :] * inputs.astype(jnp.float32)
    activation = jax.nn.gelu(mixed_in).astype(jnp.bfloat16).reshape(batches * local_len, chan_width)
    out_width = mix_weight.shape[1]
    result = jnp.dot(
        lax.all_gather(activation, "chan", axis=1, tiled=True),
        mix_weight,
        preferred_element_type=jnp.float32,
    )
    return result.astype(jnp.bfloat16).reshape(batches, local_len, out_width)


def split_dot(left, high, low):
    left_high = left.astype(bf16)
    left_low = (left - left_high.astype(f32)).astype(bf16)
    return (
        jnp.dot(left_high, high, preferred_element_type=f32)
        + jnp.dot(left_low, high, preferred_element_type=f32)
        + jnp.dot(left_high, low, preferred_element_type=f32)
    )


def weighted_sum(terms):
    total = None
    for factor, value in terms:
        if abs(factor) < 1e-9:
            continue
        if abs(factor - 1.0) < 1e-9:
            part = value
        elif abs(factor + 1.0) < 1e-9:
            part = -value
        else:
            part = value * np.float32(factor)
        total = part if total is None else total + part
    return total


def layer_kernel(
    seq_count,
    x_hbm,
    decay_hbm,
    rotation_hbm,
    in_hbm,
    out_hbm,
    rank_hbm,
    skip_hbm,
    table_hbm,
    twist_hbm,
    mix_hbm,
    result_ref,
    act_ref,
    mix_ref,
    x_ref,
    skip_ref,
    table_ref,
    twist_ref,
    turned,
    swapped,
    params_raw,
    params_own,
    omega_ref,
    weight_ref,
    decay_pairs,
    rotation_pairs,
    sums_ref,
    leaving,
    arrived,
    load_sem,
    send_in,
    recv_in,
    send_out,
    recv_out,
    send_act,
    recv_act,
):
    local_len, width = x_hbm.shape
    sub_width = width // seq_count
    states = params_raw.shape[1]
    length_all = local_len * seq_count
    half = seq_count // 2
    chunks = sub_width // CHUNK
    blocks = omega_ref.shape[0] // LANES
    group_width = 2 * LANES
    groups = width // group_width
    group_sources = group_width // sub_width
    me = lax.axis_index("seq")
    core = lax.axis_index("chan")
    other = 1 - core

    x_load = pltpu.make_async_copy(x_hbm, x_ref, load_sem.at[5])
    x_load.start()
    barrier = pltpu.get_barrier_semaphore()

    def greet(step, carry):
        pl.semaphore_signal(
            barrier,
            inc=1,
            device_id=(lax.rem(me + step, seq_count), core),
            device_id_type=MESH,
        )
        return carry

    lax.fori_loop(1, seq_count, greet, 0)
    pl.semaphore_signal(barrier, inc=1, device_id=(me, other), device_id_type=MESH)

    start = me * sub_width
    around = pl.ds(pl.multiple_of(start // LANES * LANES, LANES), LANES)
    inside = pl.ds(pl.multiple_of(lax.rem(start, LANES), sub_width), sub_width)
    loads = [
        pltpu.make_async_copy(decay_hbm.at[:, around], params_raw.at[0], load_sem.at[0]),
        pltpu.make_async_copy(rotation_hbm.at[:, around], params_raw.at[1], load_sem.at[1]),
        pltpu.make_async_copy(in_hbm.at[:, :, around], params_raw.at[2:4], load_sem.at[2]),
        pltpu.make_async_copy(out_hbm.at[:, :, around], params_raw.at[4:6], load_sem.at[3]),
        pltpu.make_async_copy(rank_hbm.at[:, :, around], params_raw.at[6:8], load_sem.at[4]),
    ]
    late_loads = [
        pltpu.make_async_copy(skip_hbm, skip_ref, load_sem.at[6]),
        pltpu.make_async_copy(table_hbm, table_ref, load_sem.at[7]),
        pltpu.make_async_copy(twist_hbm, twist_ref, load_sem.at[8]),
    ]
    mix_load = pltpu.make_async_copy(mix_hbm, mix_ref, load_sem.at[9])
    for load in loads + late_loads:
        load.start()
    mix_load.start()
    x_load.wait()

    signal_here = x_ref[...].astype(f32)
    turned[...] = jnp.transpose(signal_here).astype(bf16).reshape(turned.shape)
    swapped[me] = turned[me]

    unit = np.float32(2.0 * math.pi / length_all)
    place = lax.broadcasted_iota(jnp.int32, (LANES, LANES), 0)
    for block in range(seq_count):
        shift = (0, half)[block] if block < 2 else block // 2
        index = shift + seq_count * place
        signed = jnp.where(index < length_all // 2, index, index - length_all)
        omega = signed.astype(f32) * unit
        if block >= 2 and block % 2 == 1:
            omega = -omega
        omega_ref[block * LANES : (block + 1) * LANES, :] = omega

    for load in loads:
        load.wait()
    for kind in range(4):
        params_own[kind] = jnp.transpose(params_raw[2 * kind : 2 * kind + 2].reshape(LANES, LANES))
    own = [params_own[kind, inside, :] for kind in range(4)]
    (decay, rotation), (in_real, in_imag), (out_real, out_imag), (rank_real, rank_imag) = [
        (value[:, :states], value[:, states:]) for value in own
    ]
    scale = jnp.sqrt(2.0 * decay)
    in_real, in_imag = scale * in_real, scale * in_imag
    rank_real, rank_imag = scale * rank_real, scale * rank_imag
    reals = [
        out_real * in_real - out_imag * in_imag,
        out_real * rank_real - out_imag * rank_imag,
        rank_real * in_real + rank_imag * in_imag,
        rank_real * rank_real + rank_imag * rank_imag,
    ]
    imags = [
        out_real * in_imag + out_imag * in_real,
        out_real * rank_imag + out_imag * rank_real,
        rank_real * in_imag - rank_imag * in_real,
        jnp.zeros_like(rank_real),
    ]
    zero = jnp.zeros((PAIRS, states), f32)
    for chunk in range(chunks):
        top = slice(chunk * CHUNK, chunk * CHUNK + PAIRS)
        low = slice(chunk * CHUNK + PAIRS, (chunk + 1) * CHUNK)
        rows = slice(chunk * PAIRS, (chunk + 1) * PAIRS)
        decay_pairs[rows, :] = jnp.concatenate([decay[top], decay[low]], axis=1)
        rotation_pairs[rows, :] = jnp.concatenate([rotation[top], rotation[low]], axis=1)
        for term in range(4):
            lines = (
                (reals[term] * decay, imags[term]),
                (imags[term] * decay, -reals[term]),
            )
            for part in range(2):
                for side in range(2):
                    row = side * 8 + term * 2 + part
                    for kind in range(2):
                        value = lines[part][kind]
                        packed = (
                            jnp.concatenate([value[top], zero], axis=1)
                            if side == 0
                            else jnp.concatenate([zero, value[low]], axis=1)
                        )
                        weight_ref[kind, pl.ds(chunk * PAIRS * 16 + row, PAIRS, stride=16), :] = packed

    tile = 2 * LANES

    def one_pair(pair, carry):
        base = pl.multiple_of(pair * 16, 16)
        chunk = pair // PAIRS
        line = lax.rem(pair, PAIRS)
        weight = jnp.concatenate(
            [weight_ref[0, pl.ds(base, 16), :], weight_ref[1, pl.ds(base, 16), :]], axis=1
        )
        high = weight.astype(bf16)
        low = (weight - high.astype(f32)).astype(bf16)
        both = jnp.concatenate([high, low], axis=0)
        damp = decay_pairs[pl.ds(pair, 1), :]
        turn = rotation_pairs[pl.ds(pair, 1), :]
        damp = damp * damp
        for step in range(blocks // 2):
            offset = omega_ref[step * tile : (step + 1) * tile, :] - turn
            inverse = 1.0 / (damp + offset * offset)
            factors = jnp.concatenate(
                [inverse.astype(bf16), (offset * inverse).astype(bf16)], axis=1
            )
            sums = lax.dot_general(
                both, factors, (((1,), (1,)), ((), ())), preferred_element_type=f32
            )
            sums = sums[:16] + sums[16:]
            first = chunk * blocks + 2 * step
            sums_ref[first, pl.ds(line, 16, stride=PAIRS), :] = sums[:, :LANES]
            sums_ref[first + 1, pl.ds(line, 16, stride=PAIRS), :] = sums[:, LANES:]
        return carry

    early = chunks * PAIRS // 2
    lax.fori_loop(0, early, one_pair, 0)
    pl.semaphore_wait(barrier, seq_count)

    def in_copy(dest, source):
        return pltpu.make_async_remote_copy(
            src_ref=turned.at[dest],
            dst_ref=swapped.at[source],
            send_sem=send_in.at[dest],
            recv_sem=recv_in.at[source],
            device_id=(dest, core),
            device_id_type=MESH,
        )

    def send_inputs(step, carry):
        in_copy(lax.rem(me + step, seq_count), me).start()
        return carry

    lax.fori_loop(1, seq_count, send_inputs, 0)

    lax.fori_loop(early, chunks * PAIRS, one_pair, 0)

    def out_copy(dest, source, chunk):
        return pltpu.make_async_remote_copy(
            src_ref=leaving.at[chunk, dest],
            dst_ref=arrived.at[chunk, source],
            send_sem=send_out.at[chunk, dest],
            recv_sem=recv_out.at[chunk, source],
            device_id=(dest, core),
            device_id_type=MESH,
        )

    for chunk in range(chunks):

        def spectrum_of(block, chunk=chunk):
            reals_out, imags_out = [], []
            for side in range(2):

                def part(which, side=side):
                    row = (side * 8 + which) * PAIRS
                    return sums_ref[chunk * blocks + block, row : row + PAIRS, :]

                numer_real = part(2) * part(4) - part(3) * part(5)
                numer_imag = part(2) * part(5) + part(3) * part(4)
                denom_real = 1.0 + part(6)
                denom_imag = part(7)
                size = 1.0 / (denom_real * denom_real + denom_imag * denom_imag)
                reals_out.append(part(0) - (numer_real * denom_real + numer_imag * denom_imag) * size)
                imags_out.append(part(1) - (numer_imag * denom_real - numer_real * denom_imag) * size)
            return jnp.concatenate(reals_out, axis=0), jnp.concatenate(imags_out, axis=0)

        if chunk == 0:

            def await_inputs(step, carry):
                source = lax.rem(me + step, seq_count)
                in_copy(source, source).wait_recv()
                return carry

            lax.fori_loop(1, seq_count, await_inputs, 0)
            for load in late_loads:
                load.wait()

        signal = [
            swapped[a, chunk * CHUNK : (chunk + 1) * CHUNK, :].astype(f32) for a in range(seq_count)
        ]
        evens = [signal[a] + signal[seq_count - a] for a in range(1, half)]
        odds = [signal[a] - signal[seq_count - a] for a in range(1, half)]
        rows = []
        for c in range(half + 1):
            angles = [2.0 * math.pi * (c * a % seq_count) / seq_count for a in range(seq_count)]
            first_real = weighted_sum(
                [(1.0, signal[0]), ((-1.0) ** c, signal[half])]
                + [(math.cos(angles[a]), evens[a - 1]) for a in range(1, half)]
            )
            first_imag = weighted_sum([(-math.sin(angles[a]), odds[a - 1]) for a in range(1, half)])
            if c == 0:
                rows.append(jnp.concatenate([first_real, jnp.zeros_like(first_real)], axis=1))
                continue
            twist_cos, twist_sin = twist_ref[0, c : c + 1, :], twist_ref[1, c : c + 1, :]
            if first_imag is None:
                rows.append(jnp.concatenate([first_real * twist_cos, -first_real * twist_sin], axis=1))
            else:
                rows.append(
                    jnp.concatenate(
                        [
                            first_real * twist_cos + first_imag * twist_sin,
                            first_imag * twist_cos - first_real * twist_sin,
                        ],
                        axis=1,
                    )
                )
        freq = split_dot(jnp.concatenate(rows, axis=0), table_ref[0], table_ref[1])

        rows = []
        for c in range(half + 1):
            if c == 0 or c == half:
                spec_real, spec_imag = spectrum_of(0 if c == 0 else 1)
            else:
                ahead_real, ahead_imag = spectrum_of(2 * c)
                mirror_real, mirror_imag = spectrum_of(2 * c + 1)
                spec_real, spec_imag = ahead_real + mirror_real, ahead_imag - mirror_imag
            freq_real = freq[c * CHUNK : (c + 1) * CHUNK, :LANES]
            freq_imag = freq[c * CHUNK : (c + 1) * CHUNK, LANES:]
            rows.append(
                jnp.concatenate(
                    [
                        freq_real * spec_real - freq_imag * spec_imag,
                        freq_real * spec_imag + freq_imag * spec_real,
                    ],
                    axis=1,
                )
            )
        back = split_dot(jnp.concatenate(rows, axis=0), table_ref[2], table_ref[3])
        back_real, back_imag = [], []
        for c in range(half + 1):
            real = back[c * CHUNK : (c + 1) * CHUNK, :LANES]
            imag = back[c * CHUNK : (c + 1) * CHUNK, LANES:]
            if c > 0:
                twist_cos, twist_sin = twist_ref[0, c : c + 1, :], twist_ref[1, c : c + 1, :]
                real, imag = real * twist_cos - imag * twist_sin, imag * twist_cos + real * twist_sin
            back_real.append(real)
            back_imag.append(imag)
        shrink = np.float32(1.0 / length_all)
        for a in range(half + 1):
            angles = [2.0 * math.pi * (c * a % seq_count) / seq_count for c in range(half + 1)]
            even = weighted_sum([(math.cos(angles[c]), back_real[c]) for c in range(half + 1)])
            odd = weighted_sum([(math.sin(angles[c]), back_imag[c]) for c in range(half + 1)])
            if odd is None:
                leaving[chunk, a] = (even * shrink).astype(bf16)
            else:
                leaving[chunk, a] = ((even - odd) * shrink).astype(bf16)
                leaving[chunk, seq_count - a] = ((even + odd) * shrink).astype(bf16)

        arrived[chunk, me] = leaving[chunk, me]

        def send_results(step, carry, chunk=chunk):
            out_copy(lax.rem(me + step, seq_count), me, chunk).start()
            return carry

        lax.fori_loop(1, seq_count, send_results, 0)

    def act_copy(group, owner):
        columns = pl.ds(pl.multiple_of(owner * width + group * group_width, group_width), group_width)
        return pltpu.make_async_remote_copy(
            src_ref=act_ref.at[:, columns],
            dst_ref=act_ref.at[:, columns],
            send_sem=send_act.at[group],
            recv_sem=recv_act.at[group],
            device_id=(me, other),
            device_id_type=MESH,
        )

    nearest = me // group_sources
    for turn in range(groups):
        group = lax.rem(nearest + turn, groups)
        first = group * group_sources

        def await_results(step, carry, first=first):
            source = first + step

            @pl.when(source != me)
            def _():
                for chunk in range(chunks):
                    out_copy(source, source, chunk).wait_recv()

            return carry

        lax.fori_loop(0, group_sources, await_results, 0)
        columns = pl.ds(pl.multiple_of(group * group_width, group_width), group_width)
        stack = [
            arrived[chunk, first + source].astype(f32)
            for source in range(group_sources)
            for chunk in range(chunks)
        ]
        home = jnp.transpose(jnp.concatenate(stack, axis=0))
        mixed_in = home + skip_ref[:, columns] * x_ref[:, columns].astype(f32)
        place = pl.ds(pl.multiple_of(core * width + group * group_width, group_width), group_width)
        act_ref[:, place] = jax.nn.gelu(mixed_in).astype(bf16)
        act_copy(group, core).start()

    def mix_part(owner, group):
        place = pl.ds(pl.multiple_of(owner * width + group * group_width, group_width), group_width)
        return jnp.dot(act_ref[:, place], mix_ref[place, :], preferred_element_type=f32)

    mix_load.wait()
    total = mix_part(core, 0)
    for group in range(1, groups):
        total += mix_part(core, group)
    for turn in range(groups):
        group = lax.rem(nearest + turn, groups)
        act_copy(group, other).wait_recv()
        total += mix_part(other, group)
    result_ref[...] = total.astype(bf16)
    for group in range(groups):
        act_copy(group, core).wait_send()

    def drain(step, carry):
        dest = lax.rem(me + step, seq_count)
        in_copy(dest, dest).wait_send()
        for chunk in range(chunks):
            out_copy(dest, dest, chunk).wait_send()
        return carry

    lax.fori_loop(1, seq_count, drain, 0)


def fourier_tables(seq_count, local_len):
    place = np.arange(local_len)
    angle = 2.0 * np.pi * (np.outer(place, place) % local_len) / local_len
    cos, sin = np.cos(angle), np.sin(angle)
    ahead = np.block([[cos, -sin], [sin, cos]]).astype(np.float32)
    back = np.block([[cos, sin], [-sin, cos]]).astype(np.float32)
    parts = []
    for table in (ahead, back):
        high = table.astype(jnp.bfloat16)
        parts += [high, (table - high.astype(np.float32)).astype(jnp.bfloat16)]
    twist = 2.0 * np.pi * np.outer(np.arange(seq_count // 2 + 1), place) / (seq_count * local_len)
    return np.stack(parts), np.stack([np.cos(twist), np.sin(twist)]).astype(np.float32)


def fused_device(inputs, decay, rotation, in_proj, out_proj, low_rank, skip, mix_weight):
    _, local_len, width = inputs.shape
    seq_count = lax.axis_size("seq")
    states = decay.shape[1]
    sub_width = width // seq_count
    chunks = sub_width // CHUNK
    group_width = 2 * LANES
    groups = width // group_width
    length_all = seq_count * local_len
    tables, twist = fourier_tables(seq_count, local_len)
    whole = pl.BlockSpec(memory_space=pltpu.VMEM)
    left = pl.BlockSpec(memory_space=pltpu.HBM)
    dma = pltpu.SemaphoreType.DMA
    result = pl.pallas_call(
        functools.partial(layer_kernel, seq_count),
        out_shape=jax.ShapeDtypeStruct((local_len, mix_weight.shape[1]), bf16),
        in_specs=[left] * 10,
        out_specs=whole,
        scratch_shapes=[
            pltpu.VMEM((local_len, 2 * width), bf16),
            pltpu.VMEM(mix_weight.shape, bf16),
            pltpu.VMEM((local_len, width), bf16),
            pltpu.VMEM((1, width), f32),
            pltpu.VMEM(tables.shape, bf16),
            pltpu.VMEM(twist.shape, f32),
            pltpu.VMEM((seq_count, sub_width, local_len), bf16),
            pltpu.VMEM((seq_count, sub_width, local_len), bf16),
            pltpu.VMEM((8, states, LANES), f32),
            pltpu.VMEM((4, LANES, LANES), f32),
            pltpu.VMEM((length_all, LANES), f32),
            pltpu.VMEM((2, chunks * PAIRS * 16, LANES), f32),
            pltpu.VMEM((chunks * PAIRS, LANES), f32),
            pltpu.VMEM((chunks * PAIRS, LANES), f32),
            pltpu.VMEM((chunks * seq_count, 16 * PAIRS, LANES), f32),
            pltpu.VMEM((chunks, seq_count, CHUNK, local_len), bf16),
            pltpu.VMEM((chunks, seq_count, CHUNK, local_len), bf16),
            dma((10,)),
            dma((seq_count,)),
            dma((seq_count,)),
            dma((chunks, seq_count)),
            dma((chunks, seq_count)),
            dma((groups,)),
            dma((groups,)),
        ],
        compiler_params=pltpu.CompilerParams(collective_id=0, has_side_effects=True),
    )(
        inputs[0],
        decay.T,
        rotation.T,
        jnp.swapaxes(in_proj, 1, 2),
        jnp.swapaxes(out_proj, 1, 2),
        jnp.swapaxes(low_rank, 1, 2),
        skip.reshape(1, width),
        jnp.asarray(tables),
        jnp.asarray(twist),
        mix_weight,
    )
    return result[None]


def per_device(inputs, decay, rotation, in_proj, out_proj, low_rank, skip, mix_weight):
    batches, local_len, width = inputs.shape
    seq_count = lax.axis_size("seq")
    states = decay.shape[1]
    sub_width = width // seq_count
    fits = (
        batches == 1
        and lax.axis_size("chan") == 2
        and local_len == LANES
        and 2 * states == LANES
        and seq_count % 2 == 0
        and 2 < seq_count <= 32
        and width % (2 * LANES) == 0
        and sub_width > 0
        and sub_width % CHUNK == 0
        and LANES % sub_width == 0
    )
    run = fused_device if fits else general_device
    return run(inputs, decay, rotation, in_proj, out_proj, low_rank, skip, mix_weight)


def solution(mesh):
    return jax.shard_map(
        per_device,
        mesh=mesh,
        in_specs=(
            P(None, "seq", "chan"),
            P("chan", None),
            P("chan", None),
            P(None, "chan", None),
            P(None, "chan", None),
            P(None, "chan", None),
            P("chan"),
            P(None, "chan"),
        ),
        out_specs=P(None, "seq", "chan"),
        check_vma=False,
    )
```

profile of v0, /device:TPU:1, one launch (start us, length us, event | category | flops | bytes accessed | tf_op | source)
XLA Modules:
  0.0 23.3 jit_solution(6222824677765608751)
XLA Ops:
  0.0 21.8 %shard_map.100 = bf16[128,512]{1,0:T(8,128)(2,1)} custom-call(bf16[128,512]{1,0:T(8,128)(2,1)} %bitcast.12, f32[64,512]{1,0:T(8,128)} %bitcast.13, f32[64,512]{1,0:T(8,128)} %bitcast.14, f32[2,64,512]{2,1,0:T(8,128)} %bitcast.9, f32[2,64,512]{2,1,0:T(8,128)} %bitcast.10, f32[2,64,512]{2,1,0:T(8,128)} %bitcast.11, f32[1,512]{1,0:T(1,128)} %bitcast.15, ...), custom_call_target="tpu_custom_call" | custom-call | tf_op jit(solution)/shard_map/pallas_call | solution.py:615
  21.8 1.6 %copy.12 = bf16[1,128,512]{2,1,0:T(8,128)(2,1)} copy(bf16[1,128,512]{2,1,0:T(8,128)(2,1)} %bitcast.8) | data formatting | bytes 262144
where the time goes:
time: 23.5 us; the launch traced here: 23.3 us
  Pallas kernels  21.8 us (93%)
  local copies, waits for them, and re-layouts  1.57 us (7%)
    pallas_call x1, Pallas kernels, fused_device(): pl.pallas_call(functools.partial(layer_kernel, seq_count), out_shape=jax....  21.8 us
    unnamed x1, local copies, waits for them, and re-layouts  1.57 us

commit v1 on v0

--- a/solution.py
+++ b/solution.py
@@ -250,7 +250,7 @@
     core = lax.axis_index("chan")
     other = 1 - core
 
-    x_load = pltpu.make_async_copy(x_hbm, x_ref, load_sem.at[5])
+    x_load = pltpu.make_async_copy(x_hbm, x_ref, load_sem.at[1])
     x_load.start()
     barrier = pltpu.get_barrier_semaphore()
 
@@ -271,17 +271,17 @@
     inside = pl.ds(pl.multiple_of(lax.rem(start, LANES), sub_width), sub_width)
     loads = [
         pltpu.make_async_copy(decay_hbm.at[:, around], params_raw.at[0], load_sem.at[0]),
-        pltpu.make_async_copy(rotation_hbm.at[:, around], params_raw.at[1], load_sem.at[1]),
-        pltpu.make_async_copy(in_hbm.at[:, :, around], params_raw.at[2:4], load_sem.at[2]),
-        pltpu.make_async_copy(out_hbm.at[:, :, around], params_raw.at[4:6], load_sem.at[3]),
-        pltpu.make_async_copy(rank_hbm.at[:, :, around], params_raw.at[6:8], load_sem.at[4]),
+        pltpu.make_async_copy(rotation_hbm.at[:, around], params_raw.at[1], load_sem.at[0]),
+        pltpu.make_async_copy(in_hbm.at[:, :, around], params_raw.at[2:4], load_sem.at[0]),
+        pltpu.make_async_copy(out_hbm.at[:, :, around], params_raw.at[4:6], load_sem.at[0]),
+        pltpu.make_async_copy(rank_hbm.at[:, :, around], params_raw.at[6:8], load_sem.at[0]),
     ]
     late_loads = [
-        pltpu.make_async_copy(skip_hbm, skip_ref, load_sem.at[6]),
-        pltpu.make_async_copy(table_hbm, table_ref, load_sem.at[7]),
-        pltpu.make_async_copy(twist_hbm, twist_ref, load_sem.at[8]),
+        pltpu.make_async_copy(skip_hbm, skip_ref, load_sem.at[2]),
+        pltpu.make_async_copy(table_hbm, table_ref, load_sem.at[3]),
+        pltpu.make_async_copy(twist_hbm, twist_ref, load_sem.at[4]),
     ]
-    mix_load = pltpu.make_async_copy(mix_hbm, mix_ref, load_sem.at[9])
+    mix_load = pltpu.make_async_copy(mix_hbm, mix_ref, load_sem.at[5])
     for load in loads + late_loads:
         load.start()
     mix_load.start()
@@ -302,8 +302,7 @@
             omega = -omega
         omega_ref[block * LANES : (block + 1) * LANES, :] = omega
 
-    for load in loads:
-        load.wait()
+    pltpu.make_async_copy(params_raw, params_raw, load_sem.at[0]).wait()
     for kind in range(4):
         params_own[kind] = jnp.transpose(params_raw[2 * kind : 2 * kind + 2].reshape(LANES, LANES))
     own = [params_own[kind, inside, :] for kind in range(4)]
@@ -387,8 +386,8 @@
         return pltpu.make_async_remote_copy(
             src_ref=turned.at[dest],
             dst_ref=swapped.at[source],
-            send_sem=send_in.at[dest],
-            recv_sem=recv_in.at[source],
+            send_sem=send_in.at[0],
+            recv_sem=recv_in.at[0],
             device_id=(dest, core),
             device_id_type=MESH,
         )
@@ -400,13 +399,15 @@
     lax.fori_loop(1, seq_count, send_inputs, 0)
 
     lax.fori_loop(early, chunks * PAIRS, one_pair, 0)
+
+    nearest = me // group_sources
 
     def out_copy(dest, source, chunk):
         return pltpu.make_async_remote_copy(
             src_ref=leaving.at[chunk, dest],
             dst_ref=arrived.at[chunk, source],
-            send_sem=send_out.at[chunk, dest],
-            recv_sem=recv_out.at[chunk, source],
+            send_sem=send_out.at[0],
+            recv_sem=recv_out.at[source // group_sources],
             device_id=(dest, core),
             device_id_type=MESH,
         )
@@ -432,12 +433,8 @@
 
         if chunk == 0:
 
-            def await_inputs(step, carry):
-                source = lax.rem(me + step, seq_count)
-                in_copy(source, source).wait_recv()
-                return carry
-
-            lax.fori_loop(1, seq_count, await_inputs, 0)
+            others = swapped.at[1:]
+            pltpu.make_async_copy(others, others, recv_in.at[0]).wait()
             for load in late_loads:
                 load.wait()
 
@@ -512,7 +509,9 @@
                 leaving[chunk, a] = ((even - odd) * shrink).astype(bf16)
                 leaving[chunk, seq_count - a] = ((even + odd) * shrink).astype(bf16)
 
-        arrived[chunk, me] = leaving[chunk, me]
+        pltpu.make_async_copy(
+            leaving.at[chunk, me], arrived.at[chunk, me], recv_out.at[nearest]
+        ).start()
 
         def send_results(step, carry, chunk=chunk):
             out_copy(lax.rem(me + step, seq_count), me, chunk).start()
@@ -531,22 +530,12 @@
             device_id_type=MESH,
         )
 
-    nearest = me // group_sources
     for turn in range(groups):
         group = lax.rem(nearest + turn, groups)
         first = group * group_sources
 
-        def await_results(step, carry, first=first):
-            source = first + step
-
-            @pl.when(source != me)
-            def _():
-                for chunk in range(chunks):
-                    out_copy(source, source, chunk).wait_recv()
-
-            return carry
-
-        lax.fori_loop(0, group_sources, await_results, 0)
+        landed = arrived.at[:, pl.ds(first, group_sources)]
+        pltpu.make_async_copy(landed, landed, recv_out.at[group]).wait()
         columns = pl.ds(pl.multiple_of(group * group_width, group_width), group_width)
         stack = [
             arrived[chunk, first + source].astype(f32)
@@ -575,14 +564,9 @@
     for group in range(groups):
         act_copy(group, core).wait_send()
 
-    def drain(step, carry):
-        dest = lax.rem(me + step, seq_count)
-        in_copy(dest, dest).wait_send()
-        for chunk in range(chunks):
-            out_copy(dest, dest, chunk).wait_send()
-        return carry
-
-    lax.fori_loop(1, seq_count, drain, 0)
+    pltpu.make_async_copy(swapped.at[1:], swapped.at[1:], send_in.at[0]).wait()
+    gone = leaving.at[:, 1:]
+    pltpu.make_async_copy(gone, gone, send_out.at[0]).wait()
 
 
 def fourier_tables(seq_count, local_len):
@@ -614,7 +598,7 @@
     dma = pltpu.SemaphoreType.DMA
     result = pl.pallas_call(
         functools.partial(layer_kernel, seq_count),
-        out_shape=jax.ShapeDtypeStruct((local_len, mix_weight.shape[1]), bf16),
+        out_shape=pltpu.VMEM((local_len, mix_weight.shape[1]), bf16),
         in_specs=[left] * 10,
         out_specs=whole,
         scratch_shapes=[
@@ -635,11 +619,11 @@
             pltpu.VMEM((chunks * seq_count, 16 * PAIRS, LANES), f32),
             pltpu.VMEM((chunks, seq_count, CHUNK, local_len), bf16),
             pltpu.VMEM((chunks, seq_count, CHUNK, local_len), bf16),
-            dma((10,)),
-            dma((seq_count,)),
-            dma((seq_count,)),
-            dma((chunks, seq_count)),
-            dma((chunks, seq_count)),
+            dma((6,)),
+            dma((1,)),
+            dma((1,)),
+            dma((1,)),
+            dma((groups,)),
             dma((groups,)),
             dma((groups,)),
         ],

time: 23.5 us -> 20.9 us (0.89)
  Pallas kernels: 21.8 us -> 20.1 us
  local copies, waits for them, and re-layouts: 1.57 us -> 0.66 us
    pallas_call x1, Pallas kernels: 21.8 us -> 20.1 us  [fused_device(): pl.pallas_call(functools.partial(layer_kernel, seq_count), out_shape=pltp...]
    unnamed x1, local copies, waits for them, and re-layouts: 1.57 us -> 0.66 us
where the time goes in v1:
time: 20.9 us; the launch traced here: 20.8 us
  Pallas kernels  20.1 us (96%)
  local copies, waits for them, and re-layouts  0.66 us (3%)
    pallas_call x1, Pallas kernels, fused_device(): pl.pallas_call(functools.partial(layer_kernel, seq_count), out_shape=pltp...  20.1 us
    unnamed x1, local copies, waits for them, and re-layouts  0.66 us

profile of v1, /device:TPU:1, one launch (start us, length us, event | category | flops | bytes accessed | tf_op | source)
XLA Modules:
  0.0 20.8 jit_solution(5197917692337830162)
XLA Ops:
  0.0 20.1 %shard_map.100 = bf16[128,512]{1,0:T(8,128)(2,1)S(1)} custom-call(bf16[128,512]{1,0:T(8,128)(2,1)} %bitcast.12, f32[64,512]{1,0:T(8,128)} %bitcast.13, f32[64,512]{1,0:T(8,128)} %bitcast.14, f32[2,64,512]{2,1,0:T(8,128)} %bitcast.9, f32[2,64,512]{2,1,0:T(8,128)} %bitcast.10, f32[2,64,512]{2,1,0:T(8,128)} %bitcast.11, f32[1,512]{1,0:T(1,128)} %bitcast.15, ...), custom_call_target="tpu_custom_call" | custom-call | tf_op jit(solution)/shard_map/pallas_call | solution.py:599
  20.1 0.7 %copy.12 = bf16[1,128,512]{2,1,0:T(8,128)(2,1)} copy(bf16[1,128,512]{2,1,0:T(8,128)(2,1)S(1)} %bitcast.8) | data formatting | bytes 262144

commit v2 on v1

--- a/solution.py
+++ b/solution.py
@@ -13,6 +13,8 @@
 CHUNK = 16
 PAIRS = CHUNK // 2
 LANES = 128
+SUMS = 16
+ROWS = 2 * SUMS
 f32 = jnp.float32
 bf16 = jnp.bfloat16
 
@@ -196,6 +198,18 @@
             part = value * np.float32(factor)
         total = part if total is None else total + part
     return total
+
+
+def combine(sums):
+    first_real, first_imag, out_real, out_imag, in_real, in_imag, loop_real, loop_imag = sums
+    numer_real = out_real * in_real - out_imag * in_imag
+    numer_imag = out_real * in_imag + out_imag * in_real
+    denom_real = 1.0 + loop_real
+    size = 1.0 / (denom_real * denom_real + loop_imag * loop_imag)
+    return (
+        first_real - (numer_real * denom_real + numer_imag * loop_imag) * size,
+        first_imag - (numer_imag * denom_real - numer_real * loop_imag) * size,
+    )
 
 
 def layer_kernel(
@@ -223,9 +237,10 @@
     params_own,
     omega_ref,
     weight_ref,
-    decay_pairs,
-    rotation_pairs,
+    damp_pairs,
+    shift_pairs,
     sums_ref,
+    spec_ref,
     leaving,
     arrived,
     load_sem,
@@ -242,7 +257,7 @@
     length_all = local_len * seq_count
     half = seq_count // 2
     chunks = sub_width // CHUNK
-    blocks = omega_ref.shape[0] // LANES
+    blocks = half + 1
     group_width = 2 * LANES
     groups = width // group_width
     group_sources = group_width // sub_width
@@ -291,16 +306,35 @@
     turned[...] = jnp.transpose(signal_here).astype(bf16).reshape(turned.shape)
     swapped[me] = turned[me]
 
+    def in_copy(dest, source):
+        return pltpu.make_async_remote_copy(
+            src_ref=turned.at[dest],
+            dst_ref=swapped.at[source],
+            send_sem=send_in.at[0],
+            recv_sem=recv_in.at[0],
+            device_id=(dest, core),
+            device_id_type=MESH,
+        )
+
+    def other_place(step):
+        return step + (step >= me).astype(jnp.int32)
+
+    def send_inputs(step, carry):
+        in_copy(other_place(seq_count - 2 - step), me).start()
+        return carry
+
+    pl.semaphore_wait(barrier, seq_count)
+    lax.fori_loop(0, seq_count - 1, send_inputs, 0)
+
     unit = np.float32(2.0 * math.pi / length_all)
-    place = lax.broadcasted_iota(jnp.int32, (LANES, LANES), 0)
-    for block in range(seq_count):
-        shift = (0, half)[block] if block < 2 else block // 2
-        index = shift + seq_count * place
-        signed = jnp.where(index < length_all // 2, index, index - length_all)
-        omega = signed.astype(f32) * unit
-        if block >= 2 and block % 2 == 1:
-            omega = -omega
-        omega_ref[block * LANES : (block + 1) * LANES, :] = omega
+
+    def omega_of(block, axis):
+        index = block + seq_count * lax.broadcasted_iota(jnp.int32, (LANES, LANES), axis)
+        return jnp.where(index < length_all // 2, index, index - length_all).astype(f32) * unit
+
+    for block in range(blocks):
+        omega = omega_of(block, 0)
+        omega_ref[block * LANES : (block + 1) * LANES, :] = omega * omega
 
     pltpu.make_async_copy(params_raw, params_raw, load_sem.at[0]).wait()
     for kind in range(4):
@@ -324,81 +358,92 @@
         rank_real * in_imag - rank_imag * in_real,
         jnp.zeros_like(rank_real),
     ]
+    damp = 2.0 * decay * rotation
+    shift = rotation * rotation - decay * decay
+    damp_square = damp * damp
+    lines = []
+    for term in range(4):
+        real, imag = reals[term], imags[term]
+        scaled_real = real * decay + imag * rotation
+        scaled_imag = imag * decay - real * rotation
+        lines += [
+            (scaled_real, -scaled_imag * damp),
+            (scaled_imag, scaled_real * damp),
+            (real, -imag * damp),
+            (imag, real * damp),
+        ]
     zero = jnp.zeros((PAIRS, states), f32)
     for chunk in range(chunks):
         top = slice(chunk * CHUNK, chunk * CHUNK + PAIRS)
         low = slice(chunk * CHUNK + PAIRS, (chunk + 1) * CHUNK)
         rows = slice(chunk * PAIRS, (chunk + 1) * PAIRS)
-        decay_pairs[rows, :] = jnp.concatenate([decay[top], decay[low]], axis=1)
-        rotation_pairs[rows, :] = jnp.concatenate([rotation[top], rotation[low]], axis=1)
-        for term in range(4):
-            lines = (
-                (reals[term] * decay, imags[term]),
-                (imags[term] * decay, -reals[term]),
-            )
-            for part in range(2):
-                for side in range(2):
-                    row = side * 8 + term * 2 + part
-                    for kind in range(2):
-                        value = lines[part][kind]
-                        packed = (
-                            jnp.concatenate([value[top], zero], axis=1)
-                            if side == 0
-                            else jnp.concatenate([zero, value[low]], axis=1)
-                        )
-                        weight_ref[kind, pl.ds(chunk * PAIRS * 16 + row, PAIRS, stride=16), :] = packed
-
-    tile = 2 * LANES
+        damp_pairs[rows, :] = jnp.concatenate([damp_square[top], damp_square[low]], axis=1)
+        shift_pairs[rows, :] = jnp.concatenate([shift[top], shift[low]], axis=1)
+        for line in range(SUMS):
+            for side in range(2):
+                for kind in range(2):
+                    value = lines[line][kind]
+                    packed = (
+                        jnp.concatenate([value[top], zero], axis=1)
+                        if side == 0
+                        else jnp.concatenate([zero, value[low]], axis=1)
+                    )
+                    row = chunk * PAIRS * ROWS + side * SUMS + line
+                    weight_ref[kind, pl.ds(row, PAIRS, stride=ROWS), :] = packed
 
     def one_pair(pair, carry):
-        base = pl.multiple_of(pair * 16, 16)
+        base = pl.multiple_of(pair * ROWS, ROWS)
         chunk = pair // PAIRS
         line = lax.rem(pair, PAIRS)
         weight = jnp.concatenate(
-            [weight_ref[0, pl.ds(base, 16), :], weight_ref[1, pl.ds(base, 16), :]], axis=1
+            [weight_ref[0, pl.ds(base, ROWS), :], weight_ref[1, pl.ds(base, ROWS), :]], axis=1
         )
         high = weight.astype(bf16)
         low = (weight - high.astype(f32)).astype(bf16)
         both = jnp.concatenate([high, low], axis=0)
-        damp = decay_pairs[pl.ds(pair, 1), :]
-        turn = rotation_pairs[pl.ds(pair, 1), :]
-        damp = damp * damp
-        for step in range(blocks // 2):
-            offset = omega_ref[step * tile : (step + 1) * tile, :] - turn
-            inverse = 1.0 / (damp + offset * offset)
+        square = damp_pairs[pl.ds(pair, 1), :]
+        turn = shift_pairs[pl.ds(pair, 1), :]
+        for first in range(0, blocks, 2):
+            count = min(2, blocks - first)
+            offset = omega_ref[first * LANES : (first + count) * LANES, :] - turn
+            inverse = 1.0 / (square + offset * offset)
             factors = jnp.concatenate(
-                [inverse.astype(bf16), (offset * inverse).astype(bf16)], axis=1
+                [(offset * inverse).astype(bf16), inverse.astype(bf16)], axis=1
             )
             sums = lax.dot_general(
                 both, factors, (((1,), (1,)), ((), ())), preferred_element_type=f32
             )
-            sums = sums[:16] + sums[16:]
-            first = chunk * blocks + 2 * step
-            sums_ref[first, pl.ds(line, 16, stride=PAIRS), :] = sums[:, :LANES]
-            sums_ref[first + 1, pl.ds(line, 16, stride=PAIRS), :] = sums[:, LANES:]
+            sums = sums[:ROWS] + sums[ROWS:]
+            for block in range(count):
+                sums_ref[chunk * blocks + first + block, pl.ds(line, ROWS, stride=PAIRS), :] = sums[
+                    :, block * LANES : (block + 1) * LANES
+                ]
         return carry
 
-    early = chunks * PAIRS // 2
-    lax.fori_loop(0, early, one_pair, 0)
-    pl.semaphore_wait(barrier, seq_count)
-
-    def in_copy(dest, source):
-        return pltpu.make_async_remote_copy(
-            src_ref=turned.at[dest],
-            dst_ref=swapped.at[source],
-            send_sem=send_in.at[0],
-            recv_sem=recv_in.at[0],
-            device_id=(dest, core),
-            device_id_type=MESH,
-        )
-
-    def send_inputs(step, carry):
-        in_copy(lax.rem(me + step, seq_count), me).start()
-        return carry
-
-    lax.fori_loop(1, seq_count, send_inputs, 0)
-
-    lax.fori_loop(early, chunks * PAIRS, one_pair, 0)
+    lax.fori_loop(0, chunks * PAIRS, one_pair, 0)
+
+    for block in range(blocks):
+        omega = omega_of(block, 1)[:PAIRS]
+        for chunk in range(chunks):
+            for side in range(2):
+
+                def part(which, side=side, block=block, chunk=chunk):
+                    row = (side * SUMS + which) * PAIRS
+                    return sums_ref[chunk * blocks + block, row : row + PAIRS, :]
+
+                ahead, behind = [], []
+                for term in range(4):
+                    real, imag = part(4 * term), part(4 * term + 1)
+                    turn_real, turn_imag = omega * part(4 * term + 3), omega * part(4 * term + 2)
+                    ahead += [real + turn_real, imag - turn_imag]
+                    behind += [real - turn_real, imag + turn_imag]
+                spec_real, spec_imag = combine(ahead)
+                if 0 < block < half:
+                    mirror_real, mirror_imag = combine(behind)
+                    spec_real, spec_imag = spec_real + mirror_real, spec_imag - mirror_imag
+                lanes = slice(side * PAIRS, (side + 1) * PAIRS)
+                spec_ref[chunk, block, lanes, :LANES] = spec_real
+                spec_ref[chunk, block, lanes, LANES:] = spec_imag
 
     nearest = me // group_sources
 
@@ -413,24 +458,6 @@
         )
 
     for chunk in range(chunks):
-
-        def spectrum_of(block, chunk=chunk):
-            reals_out, imags_out = [], []
-            for side in range(2):
-
-                def part(which, side=side):
-                    row = (side * 8 + which) * PAIRS
-                    return sums_ref[chunk * blocks + block, row : row + PAIRS, :]
-
-                numer_real = part(2) * part(4) - part(3) * part(5)
-                numer_imag = part(2) * part(5) + part(3) * part(4)
-                denom_real = 1.0 + part(6)
-                denom_imag = part(7)
-                size = 1.0 / (denom_real * denom_real + denom_imag * denom_imag)
-                reals_out.append(part(0) - (numer_real * denom_real + numer_imag * denom_imag) * size)
-                imags_out.append(part(1) - (numer_imag * denom_real - numer_real * denom_imag) * size)
-            return jnp.concatenate(reals_out, axis=0), jnp.concatenate(imags_out, axis=0)
-
         if chunk == 0:
 
             others = swapped.at[1:]
@@ -471,12 +498,7 @@
 
         rows = []
         for c in range(half + 1):
-            if c == 0 or c == half:
-                spec_real, spec_imag = spectrum_of(0 if c == 0 else 1)
-            else:
-                ahead_real, ahead_imag = spectrum_of(2 * c)
-                mirror_real, mirror_imag = spectrum_of(2 * c + 1)
-                spec_real, spec_imag = ahead_real + mirror_real, ahead_imag - mirror_imag
+            spec_real, spec_imag = spec_ref[chunk, c, :, :LANES], spec_ref[chunk, c, :, LANES:]
             freq_real = freq[c * CHUNK : (c + 1) * CHUNK, :LANES]
             freq_imag = freq[c * CHUNK : (c + 1) * CHUNK, LANES:]
             rows.append(
@@ -514,10 +536,10 @@
         ).start()
 
         def send_results(step, carry, chunk=chunk):
-            out_copy(lax.rem(me + step, seq_count), me, chunk).start()
+            out_copy(other_place(step), me, chunk).start()
             return carry
 
-        lax.fori_loop(1, seq_count, send_results, 0)
+        lax.fori_loop(0, seq_count - 1, send_results, 0)
 
     def act_copy(group, owner):
         columns = pl.ds(pl.multiple_of(owner * width + group * group_width, group_width), group_width)
@@ -591,7 +613,7 @@
     chunks = sub_width // CHUNK
     group_width = 2 * LANES
     groups = width // group_width
-    length_all = seq_count * local_len
+    blocks = seq_count // 2 + 1
     tables, twist = fourier_tables(seq_count, local_len)
     whole = pl.BlockSpec(memory_space=pltpu.VMEM)
     left = pl.BlockSpec(memory_space=pltpu.HBM)
@@ -612,11 +634,12 @@
             pltpu.VMEM((seq_count, sub_width, local_len), bf16),
             pltpu.VMEM((8, states, LANES), f32),
             pltpu.VMEM((4, LANES, LANES), f32),
-            pltpu.VMEM((length_all, LANES), f32),
-            pltpu.VMEM((2, chunks * PAIRS * 16, LANES), f32),
+            pltpu.VMEM((blocks * LANES, LANES), f32),
+            pltpu.VMEM((2, chunks * PAIRS * ROWS, LANES), f32),
             pltpu.VMEM((chunks * PAIRS, LANES), f32),
             pltpu.VMEM((chunks * PAIRS, LANES), f32),
-            pltpu.VMEM((chunks * seq_count, 16 * PAIRS, LANES), f32),
+            pltpu.VMEM((chunks * blocks, ROWS * PAIRS, LANES), f32),
+            pltpu.VMEM((chunks, blocks, CHUNK, 2 * LANES), f32),
             pltpu.VMEM((chunks, seq_count, CHUNK, local_len), bf16),
             pltpu.VMEM((chunks, seq_count, CHUNK, local_len), bf16),
             dma((6,)),

time: 20.9 us -> 19.4 us (0.928)
  Pallas kernels: 20.1 us -> 18.6 us
    pallas_call x1, Pallas kernels: 20.1 us -> 18.6 us  [fused_device(): pl.pallas_call(functools.partial(layer_kernel, seq_count), out_shape=pltp...]
where the time goes in v2:
time: 19.4 us; the launch traced here: 19.3 us
  Pallas kernels  18.6 us (96%)
  local copies, waits for them, and re-layouts  0.66 us (3%)
    pallas_call x1, Pallas kernels, fused_device(): pl.pallas_call(functools.partial(layer_kernel, seq_count), out_shape=pltp...  18.6 us
    unnamed x1, local copies, waits for them, and re-layouts  0.66 us

profile of v2, /device:TPU:1, one launch (start us, length us, event | category | flops | bytes accessed | tf_op | source)
XLA Modules:
  0.0 19.3 jit_solution(7892495985709790920)
XLA Ops:
  0.0 18.6 %shard_map.100 = bf16[128,512]{1,0:T(8,128)(2,1)S(1)} custom-call(bf16[128,512]{1,0:T(8,128)(2,1)} %bitcast.12, f32[64,512]{1,0:T(8,128)} %bitcast.13, f32[64,512]{1,0:T(8,128)} %bitcast.14, f32[2,64,512]{2,1,0:T(8,128)} %bitcast.9, f32[2,64,512]{2,1,0:T(8,128)} %bitcast.10, f32[2,64,512]{2,1,0:T(8,128)} %bitcast.11, f32[1,512]{1,0:T(1,128)} %bitcast.15, ...), custom_call_target="tpu_custom_call" | custom-call | tf_op jit(solution)/shard_map/pallas_call | solution.py:621
  18.6 0.7 %copy.12 = bf16[1,128,512]{2,1,0:T(8,128)(2,1)} copy(bf16[1,128,512]{2,1,0:T(8,128)(2,1)S(1)} %bitcast.8) | data formatting | bytes 262144

commit v3 on v2

--- a/solution.py
+++ b/solution.py
@@ -173,16 +173,6 @@
         preferred_element_type=jnp.float32,
     )
     return result.astype(jnp.bfloat16).reshape(batches, local_len, out_width)
-
-
-def split_dot(left, high, low):
-    left_high = left.astype(bf16)
-    left_low = (left - left_high.astype(f32)).astype(bf16)
-    return (
-        jnp.dot(left_high, high, preferred_element_type=f32)
-        + jnp.dot(left_low, high, preferred_element_type=f32)
-        + jnp.dot(left_high, low, preferred_element_type=f32)
-    )
 
 
 def weighted_sum(terms):
@@ -494,7 +484,9 @@
                         axis=1,
                     )
                 )
-        freq = split_dot(jnp.concatenate(rows, axis=0), table_ref[0], table_ref[1])
+        freq = jnp.dot(
+            jnp.concatenate(rows, axis=0).astype(bf16), table_ref[0], preferred_element_type=f32
+        )
 
         rows = []
         for c in range(half + 1):
@@ -510,7 +502,9 @@
                     axis=1,
                 )
             )
-        back = split_dot(jnp.concatenate(rows, axis=0), table_ref[2], table_ref[3])
+        back = jnp.dot(
+            jnp.concatenate(rows, axis=0).astype(bf16), table_ref[1], preferred_element_type=f32
+        )
         back_real, back_imag = [], []
         for c in range(half + 1):
             real = back[c * CHUNK : (c + 1) * CHUNK, :LANES]
@@ -597,12 +591,8 @@
     cos, sin = np.cos(angle), np.sin(angle)
     ahead = np.block([[cos, -sin], [sin, cos]]).astype(np.float32)
     back = np.block([[cos, sin], [-sin, cos]]).astype(np.float32)
-    parts = []
-    for table in (ahead, back):
-        high = table.astype(jnp.bfloat16)
-        parts += [high, (table - high.astype(np.float32)).astype(jnp.bfloat16)]
     twist = 2.0 * np.pi * np.outer(np.arange(seq_count // 2 + 1), place) / (seq_count * local_len)
-    return np.stack(parts), np.stack([np.cos(twist), np.sin(twist)]).astype(np.float32)
+    return np.stack([ahead, back]).astype(jnp.bfloat16), np.stack([np.cos(twist), np.sin(twist)]).astype(np.float32)
 
 
 def fused_device(inputs, decay, rotation, in_proj, out_proj, low_rank, skip, mix_weight):

time: 19.4 us -> 19.1 us (0.985)
  Pallas kernels: 18.6 us -> 18.3 us
    pallas_call x1, Pallas kernels: 18.6 us -> 18.3 us  [fused_device(): pl.pallas_call(functools.partial(layer_kernel, seq_count), out_shape=pltp...]
where the time goes in v3:
time: 19.1 us; the launch traced here: 19 us
  Pallas kernels  18.3 us (96%)
  local copies, waits for them, and re-layouts  0.66 us (3%)
    pallas_call x1, Pallas kernels, fused_device(): pl.pallas_call(functools.partial(layer_kernel, seq_count), out_shape=pltp...  18.3 us
    unnamed x1, local copies, waits for them, and re-layouts  0.66 us

profile of v3, /device:TPU:1, one launch (start us, length us, event | category | flops | bytes accessed | tf_op | source)
XLA Modules:
  0.0 19.0 jit_solution(8428994232990028802)
XLA Ops:
  0.0 18.3 %shard_map.100 = bf16[128,512]{1,0:T(8,128)(2,1)S(1)} custom-call(bf16[128,512]{1,0:T(8,128)(2,1)} %bitcast.12, f32[64,512]{1,0:T(8,128)} %bitcast.13, f32[64,512]{1,0:T(8,128)} %bitcast.14, f32[2,64,512]{2,1,0:T(8,128)} %bitcast.9, f32[2,64,512]{2,1,0:T(8,128)} %bitcast.10, f32[2,64,512]{2,1,0:T(8,128)} %bitcast.11, f32[1,512]{1,0:T(1,128)} %bitcast.15, ...), custom_call_target="tpu_custom_call" | custom-call | tf_op jit(solution)/shard_map/pallas_call | solution.py:611
  18.3 0.7 %copy.12 = bf16[1,128,512]{2,1,0:T(8,128)(2,1)} copy(bf16[1,128,512]{2,1,0:T(8,128)(2,1)S(1)} %bitcast.8) | data formatting | bytes 262144
